TPU v7x, 32 devices: a whole 2x2x4 slice. The times are simulated.
32 devices in a mesh: groups: 2 (over x), chan: 16 (over z, y, core).
Axes of the slice: x: 2, y: 2, z: 4, core: 2. Of those that a mesh axis runs over, the one named last changes fastest.
Arguments:
- data: bfloat16 [28672, 4096], P(('groups', 'chan')), parts along dimension 0, as said below
- alive: int32 [8192], P(('groups', 'chan')), parts along dimension 0, may hold values 0 or 1
- sources: int32 [2, 16], replicated, may hold values from 0 to 4095, as said below
Outputs:
- correlations: bfloat16 [4, 16, 256, 4096], P('groups', None, None, 'chan'), parts along dimension 0
There are 2 independent parts, one for each index of `groups`. A program takes and returns all parts, laid end to end along the dimension named above; an argument that names none is the same for every part. Nothing has to cross between parts.
Inputs may be any that keep to these rules, and one draw needn't show every extreme that they name: `sources`: no channel number appears twice in the array, and channel 4096 - 1 is always one of them. `data`: samples have channel and time-block scales of their own.
All inputs are finite; a program needn't handle non-finite values. No bound on the sum of `alive` on one device may be relied on, other than what follows from the above.
Results may differ from a plain program's by a relative error of at most 0.0076.
Values may be sent and summed in bfloat16 or wider, within the bound.
No kernel may reach another device: no remote copies, remote signals or barrier semaphores. Data moves between devices by JAX's collectives and lax.ppermute only.
A program may use at most 128 MiB of HBM per device.

v0:
```python
import math
import jax
import jax.numpy as jnp
from jax import lax
from jax.sharding import PartitionSpec as P

SEGMENT_LENGTH = 512
NF = 128
LAGS = 256
SRC = 16
ROUNDS = 2
SEGMENT_TALLY = 28


def forward_table():
    times = jnp.arange(SEGMENT_LENGTH, dtype=jnp.int32)[:, None]
    bins = jnp.arange(NF, dtype=jnp.int32)[None, :] + 1
    angle = 2.0 * math.pi / SEGMENT_LENGTH * (bins * times % SEGMENT_LENGTH).astype(jnp.float32)
    table = jnp.concatenate([jnp.cos(angle), -jnp.sin(angle)], axis=1) / math.sqrt(SEGMENT_LENGTH)
    return table.astype(jnp.bfloat16)


def inverse_table():
    shifts = jnp.arange(LAGS, dtype=jnp.int32)[:, None] - LAGS // 2
    bins = jnp.arange(NF, dtype=jnp.int32)[None, :] + 1
    angle = 2.0 * math.pi / SEGMENT_LENGTH * (bins * shifts % SEGMENT_LENGTH).astype(jnp.float32)
    return jnp.concatenate([jnp.cos(angle), -jnp.sin(angle)], axis=1).astype(jnp.bfloat16)


def body(data, alive, sources):
    count = lax.axis_size("chan")
    width = data.shape[1] // count
    table = forward_table()
    split = data.reshape(data.shape[0], count, width)
    moved = lax.all_to_all(split, "chan", split_axis=1, concat_axis=0, tiled=True)
    blocks = moved.reshape(SEGMENT_TALLY, SEGMENT_LENGTH, moved.shape[2])
    spectra = jnp.einsum("tk,wtc->wkc", table, blocks, preferred_element_type=jnp.float32)
    level = jnp.mean(spectra[:, :NF] ** 2 + spectra[:, NF:] ** 2, axis=0)
    factor = alive.astype(jnp.float32)[None, :] / jnp.sqrt(level + 0.01)
    factor = jnp.concatenate([factor, factor], axis=0)
    whitened = (spectra * factor[None]).astype(jnp.bfloat16)
    ids = sources.reshape(-1)
    owner = ids // width
    local = ids % width
    mine = owner == lax.axis_index("chan")
    picked = jnp.transpose(jnp.take(whitened, local, axis=2), (2, 0, 1)).astype(jnp.float32)
    picked = jnp.where(mine[:, None, None], picked, 0.0)
    src = lax.psum(picked, "chan").astype(jnp.bfloat16)
    src_re, src_im = (src[:, :, :NF], src[:, :, NF:])
    own_re, own_im = (whitened[:, :NF], whitened[:, NF:])
    form = "qwf,wfc->qfc"
    correlogram_realpart = jnp.einsum(
        form, src_re, own_re, preferred_element_type=jnp.float32
    ) + jnp.einsum(form, src_im, own_im, preferred_element_type=jnp.float32)
    cross_imaginary = jnp.einsum(
        form, src_re, own_im, preferred_element_type=jnp.float32
    ) - jnp.einsum(form, src_im, own_re, preferred_element_type=jnp.float32)
    cross = jnp.concatenate([correlogram_realpart, cross_imaginary], axis=1).astype(jnp.bfloat16)
    lagged = jnp.einsum("lk,qkc->qlc", inverse_table(), cross, preferred_element_type=jnp.float32)
    lagged = lagged / math.sqrt(NF * SEGMENT_TALLY)
    return lagged.reshape(ROUNDS, SRC, LAGS, width).astype(jnp.bfloat16)


def solution(mesh):
    return jax.shard_map(
        body,
        mesh=mesh,
        in_specs=(P(("groups", "chan"), None), P(("groups", "chan")), P()),
        out_specs=P("groups", None, None, "chan"),
        check_vma=False,
    )
```

profile of v0, /device:TPU:0, one launch (start us, length us, event | category | flops | bytes accessed | tf_op | source)
XLA Modules:
  0.0 326.9 jit_solution(7985542122648060904)
XLA Ops:
  0.0 6.9 %copy.27 = bf16[112,16,8,256]{3,2,0,1:T(8,128)(2,1)} copy(bf16[112,16,8,256]{3,2,1,0:T(8,128)(2,1)} %bitcast.32) | data formatting | bytes 14680064 | tf_op jit(solution)/shard_map/reshape | solution.py:34
  6.9 0.0 copy-start.3
  6.9 0.0 copy-start.2
  6.9 7.6 %all-to-all-start = ((bf16[896,16,256]{2,0,1:T(8,128)(2,1)}), bf16[896,16,256]{2,0,1:T(8,128)(2,1)}, u32[]{:S(2)}, u32[]{:S(2)}) async-start(bf16[896,16,256]{2,0,1:T(8,128)(2,1)} %bitcast.31), calls=%async_computation | async-start | bytes 14680064 | tf_op jit(solution)/shard_map/all_to_all | solution.py:35
  14.4 0.0 copy-done.3
  14.4 0.1 reshape.125
  14.5 0.1 reshape.124
  14.6 0.0 copy-done.2
  14.7 0.6 cosine_convert_fusion
  15.3 1.1 fusion.33
  16.4 130.5 %all-to-all-done = bf16[896,16,256]{2,0,1:T(8,128)(2,1)} async-done(((bf16[896,16,256]{2,0,1:T(8,128)(2,1)}), bf16[896,16,256]{2,0,1:T(8,128)(2,1)}, u32[]{:S(2)}, u32[]{:S(2)}) %all-to-all-start) | async-done | bytes 7340064 | tf_op jit(solution)/shard_map/all_to_all | solution.py:35
  146.9 5.2 %convolution_bitcast_fusion = f32[28,256,256]{2,1,0:T(8,128)S(1)} fusion(bf16[28,512,256]{2,1,0:T(8,128)(2,1)} %bitcast.3, f32[512,128]{0,1:T(8,128)S(1)} %get-tuple-element.14, f32[512,128]{0,1:T(8,128)S(1)} %get-tuple-element.13), kind=kOutput, calls=%fused_computation.14 | convolution fusion | flops 1879441408 | bytes 15204352 | tf_op jit(solution)/shard_map/tk,wtc->wkc/dot_general | solution.py:37
  152.0 0.5 fusion.5
  152.6 2.6 multiply_convert_fusion.1
  155.2 7.7 %copy.7 = bf16[28,256,256]{1,0,2:T(8,128)(2,1)} copy(bf16[28,256,256]{2,1,0:T(8,128)(2,1)} %multiply_convert_fusion.1) | data formatting | bytes 7340032 | tf_op jit(solution)/shard_map/convert_element_type | solution.py:41
  162.9 3.6 %fusion.40 = (bf16[28,128,256]{2,1,0:T(8,128)(2,1)S(1)}, bf16[28,128,256]{2,1,0:T(8,128)(2,1)}) fusion(bf16[28,256,256]{2,1,0:T(8,128)(2,1)} %multiply_convert_fusion.1), kind=kLoop, calls=%fused_computation.76 | loop fusion | bytes 7340032 | tf_op jit(solution)/shard_map/slice | solution.py:50
  166.6 2.8 gather_fusion
  169.3 0.2 convert_select_fusion
  169.6 100.6 %all-reduce.1 = bf16[32,28,256]{2,1,0:T(8,128)(2,1)S(1)} all-reduce(f32[32,28,256]{2,1,0:T(8,128)S(1)} %convert_select_fusion), channel_id=1, replica_groups=mesh['groups'=2,'chan'=16] {'chan'}, use_global_device_ids=true, to_apply=%region_1.2 | all-reduce | flops 229376 | bytes 1376256 | tf_op jit(solution)/shard_map/psum | solution.py:48
  270.2 0.1 fusion.41
  270.3 2.6 copy.13
  272.8 1.6 copy.10
  274.5 0.0 copy-start
  274.5 0.0 copy-start.1
  274.5 4.6 %fusion.14 = f32[128,256,32]{1,2,0:T(8,128)} fusion(bf16[32,28,128]{0,1,2:T(8,128)(2,1)} %copy.13, bf16[28,128,256]{2,1,0:T(8,128)(2,1)S(1)} %get-tuple-element.5), kind=kOutput, calls=%fused_computation.21 | convolution fusion | flops 58720256 | bytes 6258688 | tf_op jit(solution)/shard_map/qwf,wfc->qfc/dot_general | solution.py:57
  279.1 0.0 copy-done
  279.1 0.0 copy-done.1
  279.1 3.2 fusion.12
  282.4 3.3 fusion.10
  285.6 3.3 %fusion.16 = f32[128,256,32]{1,2,0:T(8,128)} fusion(bf16[32,28,128]{0,1,2:T(8,128)(2,1)S(1)} %copy.10, bf16[28,128,256]{2,1,0:T(8,128)(2,1)S(1)} %get-tuple-element.5), kind=kOutput, calls=%fused_computation.23 | convolution fusion | flops 58720256 | bytes 6258688 | tf_op jit(solution)/shard_map/qwf,wfc->qfc/dot_general | solution.py:52
  288.9 5.3 %copy.16 = f32[128,256,32]{0,1,2:T(8,128)} copy(f32[128,256,32]{1,2,0:T(8,128)} %fusion.14) | data formatting | bytes 8388608 | tf_op jit(solution)/shard_map/qwf,wfc->qfc/dot_general | solution.py:57
  294.2 5.3 %copy.15 = f32[128,256,32]{0,1,2:T(8,128)} copy(f32[128,256,32]{1,2,0:T(8,128)} %fusion.10) | data formatting | bytes 8388608 | tf_op jit(solution)/shard_map/qwf,wfc->qfc/dot_general | solution.py:55
  299.6 5.3 %copy.14 = f32[128,256,32]{0,1,2:T(8,128)} copy(f32[128,256,32]{1,2,0:T(8,128)} %fusion.12) | data formatting | bytes 8388608 | tf_op jit(solution)/shard_map/qwf,wfc->qfc/dot_general | solution.py:54
  304.9 5.3 %copy.11 = f32[128,256,32]{0,1,2:T(8,128)} copy(f32[128,256,32]{1,2,0:T(8,128)} %fusion.16) | data formatting | bytes 8388608 | tf_op jit(solution)/shard_map/qwf,wfc->qfc/dot_general | solution.py:52
  310.2 7.6 %fusion.8 = (bf16[32,128,256]{1,2,0:T(8,128)(2,1)S(1)}, bf16[32,128,256]{1,2,0:T(8,128)(2,1)S(1)}) fusion(f32[128,256,32]{0,1,2:T(8,128)} %copy.11, f32[128,256,32]{0,1,2:T(8,128)} %copy.14, f32[128,256,32]{0,1,2:T(8,128)} %copy.15, f32[128,256,32]{0,1,2:T(8,128)} %copy.16), kind=kLoop, calls=%fused_computation.15 | loop fusion | flops 4194304 | bytes 20971520 | tf_op jit(solution)/shard_map/add | solution.py:52
  317.8 2.9 multiply_convert_fusion
  320.7 6.2 %copy.8 = bf16[2,16,256,256]{3,2,1,0:T(8,128)(2,1)} copy(bf16[2,16,256,256]{2,3,1,0:T(8,128)(2,1)} %bitcast.33) | data formatting | bytes 8388608 | tf_op jit(solution)/shard_map/convert_element_type | solution.py:61
  (8 shorter events, 0.1 us)
Async XLA Ops:
  6.9 7.6 %copy-start.3 = (s32[2,16]{1,0:T(2,128)S(1)}, s32[2,16]{1,0:T(2,128)}, u32[]{:S(2)}) copy-start(s32[2,16]{1,0:T(2,128)} %param.5) | copy-start | bytes 388
  6.9 7.8 %copy-start.2 = (s32[256]{0:T(256)S(1)}, s32[256]{0:T(256)}, u32[]{:S(2)}) copy-start(s32[256]{0:T(256)} %param.4) | copy-start | bytes 3076
  6.9 140.0 %all-to-all-start = ((bf16[896,16,256]{2,0,1:T(8,128)(2,1)}), bf16[896,16,256]{2,0,1:T(8,128)(2,1)}, u32[]{:S(2)}, u32[]{:S(2)}) async-start(bf16[896,16,256]{2,0,1:T(8,128)(2,1)} %bitcast.31), calls=%async_computation | async-start | bytes 14680064 | tf_op jit(solution)/shard_map/all_to_all | solution.py:35
  274.5 4.7 %copy-start = (bf16[28,128,256]{2,1,0:T(8,128)(2,1)S(1)}, bf16[28,128,256]{2,1,0:T(8,128)(2,1)}, u32[]{:S(2)}) copy-start(bf16[28,128,256]{2,1,0:T(8,128)(2,1)} %get-tuple-element.6) | copy-start | bytes 5505028
  274.5 4.7 %copy-start.1 = (bf16[32,28,128]{0,1,2:T(8,128)(2,1)S(1)}, bf16[32,28,128]{0,1,2:T(8,128)(2,1)}, u32[]{:S(2)}) copy-start(bf16[32,28,128]{0,1,2:T(8,128)(2,1)} %copy.13) | copy-start | bytes 688132
where the time goes:
time: 328 us; the launch traced here: 327 us
  waiting for transfers between devices  130 us (40%)
  blocking collectives  101 us (31%)
  local copies, waits for them, and re-layouts  52.9 us (16%)
  matrix products  22.5 us (7%)
  other arithmetic  12.8 us (4%)
  starting transfers between devices  7.56 us (2%)
    all_to_all x1, waiting for transfers between devices, body(): lax.all_to_all(split, 'chan', split_axis=1, concat_axis=0, tiled=True)  130 us
    psum x1, blocking collectives, body(): src = lax.psum(picked, 'chan').astype(jnp.bfloat16)  101 us
    convert_element_type x1, local copies, waits for them, and re-layouts, body(): whitened = (spectra * factor[None]).astype(jnp.bfloat16)  7.7 us
    add x1, other arithmetic, body(): jnp.einsum(form, src_re, own_re, preferred_element_type=jnp.float32)  7.63 us
    all_to_all x1, starting transfers between devices, body(): lax.all_to_all(split, 'chan', split_axis=1, concat_axis=0, tiled=True)  7.56 us
    reshape x1, local copies, waits for them, and re-layouts, body(): split = data.reshape(data.shape[0], count, width)  6.85 us
  transfers between devices with their start and end apart: 1, of which 1 were waited for; matrix products, arithmetic and copies ran while one was open for 1% of the time, Pallas kernels for 0%

commit v1 on v0

--- a/solution.py
+++ b/solution.py
@@ -10,6 +10,11 @@
 SRC = 16
 ROUNDS = 2
 SEGMENT_TALLY = 28
+
+
+def add_all(x, mesh_axis):
+    shards = lax.all_gather(x, mesh_axis)
+    return jnp.sum(shards, axis=0)
 
 
 def forward_table():
@@ -45,7 +50,7 @@
     mine = owner == lax.axis_index("chan")
     picked = jnp.transpose(jnp.take(whitened, local, axis=2), (2, 0, 1)).astype(jnp.float32)
     picked = jnp.where(mine[:, None, None], picked, 0.0)
-    src = lax.psum(picked, "chan").astype(jnp.bfloat16)
+    src = add_all(picked, "chan").astype(jnp.bfloat16)
     src_re, src_im = (src[:, :, :NF], src[:, :, NF:])
     own_re, own_im = (whitened[:, :NF], whitened[:, NF:])
     form = "qwf,wfc->qfc"

time: 328 us -> 354 us (1.079)
  waiting for transfers between devices: 130 us -> 268 us
  blocking collectives: 101 us -> 0 us
  local copies, waits for them, and re-layouts: 52.9 us -> 32.7 us
  between operations: 0.16 us -> 13.5 us
    all_gather x0 -> x1, waiting for transfers between devices: none -> 137 us  [add_all(): shards = lax.all_gather(x, mesh_axis)]
    psum x1 -> x0, blocking collectives: 101 us -> none  [body(): src = lax.psum(picked, 'chan').astype(jnp.bfloat16)]
    dot_general x4 -> x0, local copies, waits for them, and re-layouts: 21.3 us -> none  [the longest x1 5.34 us: body(): jnp.einsum(form, src_re, own_im, preferred_element_type=jnp.float32)]
    add x1 -> x0, other arithmetic: 7.63 us -> none  [body(): jnp.einsum(form, src_re, own_re, preferred_element_type=jnp.float32)]
    reduce_sum x0 -> x1, other arithmetic: none -> 7.04 us  [add_all(): return jnp.sum(shards, axis=0)]
    dot_general x1, matrix products: 2.88 us -> 7.24 us  [body(): jnp.einsum('lk,qkc->qlc', inverse_table(), cross, preferred_element_type=...]
    slice x3 -> x0, local copies, waits for them, and re-layouts: 4.28 us -> none  [body(): src_re, src_im = (src[:, :, :NF], src[:, :, NF:])]
    reduce_sum x0 -> x1, local copies, waits for them, and re-layouts: none -> 4 us  [add_all(): return jnp.sum(shards, axis=0)]
  transfers between devices with their start and end apart: 1 -> 2, of which waited for: 1 -> 2; matrix products, arithmetic and copies ran while one was open for 1% -> 2% of each run, Pallas kernels for 0% -> 0%
where the time goes in v1:
time: 354 us
  waiting for transfers between devices  268 us (76%)
  local copies, waits for them, and re-layouts  32.7 us (9%)
  matrix products  19 us (5%)
  between operations  13.5 us (4%)
  other arithmetic  12.5 us (4%)
  starting transfers between devices  7.6 us (2%)
    all_gather x1, waiting for transfers between devices, add_all(): shards = lax.all_gather(x, mesh_axis)  137 us
    all_to_all x1, waiting for transfers between devices, body(): lax.all_to_all(split, 'chan', split_axis=1, concat_axis=0, tiled=True)  131 us
    convert_element_type x1, local copies, waits for them, and re-layouts, body(): whitened = (spectra * factor[None]).astype(jnp.bfloat16)  7.7 us
    all_to_all x1, starting transfers between devices, body(): lax.all_to_all(split, 'chan', split_axis=1, concat_axis=0, tiled=True)  7.56 us
    dot_general x1, matrix products, body(): jnp.einsum('lk,qkc->qlc', inverse_table(), cross, preferred_element_type=...  7.24 us
  transfers between devices with their start and end apart: 2, of which 2 were waited for; matrix products, arithmetic and copies ran while one was open for 2% of the time, Pallas kernels for 0%

profile of v1, /device:TPU:0, one launch (start us, length us, event | category | flops | bytes accessed | tf_op | source)
XLA Modules:
  0.0 353.8 jit_solution(13141758108189014661)
XLA Ops:
  6.5 6.8 %copy.38 = bf16[112,16,8,256]{3,2,0,1:T(8,128)(2,1)} copy(bf16[112,16,8,256]{3,2,1,0:T(8,128)(2,1)} %bitcast.30) | data formatting | bytes 14680064 | tf_op jit(solution)/shard_map/reshape | solution.py:39
  13.4 0.0 copy-start.3
  13.4 0.0 copy-start.2
  13.4 7.6 %all-to-all-start = ((bf16[896,16,256]{2,0,1:T(8,128)(2,1)}), bf16[896,16,256]{2,0,1:T(8,128)(2,1)}, u32[]{:S(2)}, u32[]{:S(2)}) async-start(bf16[896,16,256]{2,0,1:T(8,128)(2,1)} %bitcast.28), calls=%async_computation | async-start | bytes 14680064 | tf_op jit(solution)/shard_map/all_to_all | solution.py:40
  20.9 0.0 all-gather.3.cloned.1.call-start
  21.0 0.0 copy-done.3
  21.0 0.1 reshape.125
  21.1 0.1 reshape.124
  21.2 0.0 copy-done.2
  21.2 1.1 fusion.37
  22.3 131.1 %all-to-all-done = bf16[896,16,256]{2,0,1:T(8,128)(2,1)} async-done(((bf16[896,16,256]{2,0,1:T(8,128)(2,1)}), bf16[896,16,256]{2,0,1:T(8,128)(2,1)}, u32[]{:S(2)}, u32[]{:S(2)}) %all-to-all-start) | async-done | bytes 7340064 | tf_op jit(solution)/shard_map/all_to_all | solution.py:40
  153.4 5.2 %convolution_bitcast_fusion = f32[28,256,256]{2,1,0:T(8,128)S(1)} fusion(bf16[28,512,256]{2,1,0:T(8,128)(2,1)} %bitcast.3, f32[512,128]{0,1:T(8,128)S(1)} %get-tuple-element.12, f32[512,128]{0,1:T(8,128)S(1)} %get-tuple-element.11), kind=kOutput, calls=%fused_computation.13 | convolution fusion | flops 1879441408 | bytes 15204352 | tf_op jit(solution)/shard_map/tk,wtc->wkc/dot_general | solution.py:42
  158.5 0.5 fusion.3
  159.1 2.6 multiply_convert_fusion.1
  161.7 7.7 %copy.11 = bf16[28,256,256]{1,0,2:T(8,128)(2,1)} copy(bf16[28,256,256]{2,1,0:T(8,128)(2,1)} %multiply_convert_fusion.1) | data formatting | bytes 7340032 | tf_op jit(solution)/shard_map/convert_element_type | solution.py:46
  169.4 2.8 gather_fusion
  172.2 0.2 convert_select_fusion
  172.4 1.5 copy.12
  173.9 0.0 all-gather.3.cloned.1.call-update
  173.9 0.6 cosine_convert_fusion
  174.5 3.6 %fusion.44 = (bf16[28,128,256]{2,1,0:T(8,128)(2,1)S(1)}, bf16[28,128,256]{2,1,0:T(8,128)(2,1)}) fusion(bf16[28,256,256]{2,1,0:T(8,128)(2,1)} %multiply_convert_fusion.1), kind=kLoop, calls=%fused_computation.77 | loop fusion | bytes 7340032 | tf_op jit(solution)/shard_map/slice | solution.py:55
  178.2 137.4 %all-gather.3.cloned.1.call-done = f32[512,28,256]{2,0,1:T(8,128)} async-done(((f32[32,28,256]{2,0,1:T(8,128)}), f32[512,28,256]{2,0,1:T(8,128)}) %all-gather.3.cloned.1.call-update) | async-done | bytes 14680080 | tf_op jit(solution)/shard_map/all_gather | solution.py:16
  315.5 7.0 %reduce_sum.19 = bf16[32,28,256]{2,0,1:T(8,128)(2,1)S(1)} reduce(f32[16,32,28,256]{3,1,0,2:T(8,128)} %bitcast.29, f32[]{:T(128)} %constant.78.clone.1), dimensions={0}, to_apply=%region_1.2 | reduce | flops 3440640 | bytes 15138820 | tf_op jit(solution)/shard_map/reduce_sum | solution.py:17
  322.6 4.0 %copy.13 = bf16[32,28,256]{1,0,2:T(8,128)(2,1)} copy(bf16[32,28,256]{2,0,1:T(8,128)(2,1)S(1)} %reduce_sum.19) | data formatting | bytes 917504 | tf_op jit(solution)/shard_map/reduce_sum | solution.py:17
  326.6 0.0 copy-start
  326.6 0.0 copy-start.1
  326.6 2.6 fusion.10
  329.2 0.0 copy-done
  329.2 0.0 copy-done.1
  329.2 1.2 fusion.6
  330.4 1.3 fusion.12
  331.8 1.4 fusion.15
  333.2 0.4 pad_maximum_fusion
  333.6 7.2 %multiply_convert_fusion = bf16[32,256,256]{2,1,0:T(8,128)(2,1)} fusion(bf16[32,256,256]{2,0,1:T(8,128)(2,1)S(1)} %pad_maximum_fusion, bf16[256,128]{1,0:T(8,128)(2,1)S(1)} %get-tuple-element.8, bf16[256,128]{1,0:T(8,128)(2,1)S(1)} %get-tuple-element.7), kind=kOutput, calls=%fused_computation.1 | convolution fusion | flops 1078198272 | bytes 8519680 | tf_op jit(solution)/shard_map/lk,qkc->qlc/dot_general | solution.py:64
  340.8 6.2 %copy.19 = bf16[2,16,256,256]{3,2,1,0:T(8,128)(2,1)} copy(bf16[2,16,256,256]{2,3,1,0:T(8,128)(2,1)} %bitcast.31) | data formatting | bytes 8388608 | tf_op jit(solution)/shard_map/convert_element_type | solution.py:66
  (8 shorter events, 0.1 us)
Async XLA Ops:
  13.4 7.6 %copy-start.3 = (s32[2,16]{1,0:T(2,128)S(1)}, s32[2,16]{1,0:T(2,128)}, u32[]{:S(2)}) copy-start(s32[2,16]{1,0:T(2,128)} %param.5) | copy-start | bytes 388
  13.4 7.8 %copy-start.2 = (s32[256]{0:T(256)S(1)}, s32[256]{0:T(256)}, u32[]{:S(2)}) copy-start(s32[256]{0:T(256)} %param.4) | copy-start | bytes 3076
  13.4 140.0 %all-to-all-start = ((bf16[896,16,256]{2,0,1:T(8,128)(2,1)}), bf16[896,16,256]{2,0,1:T(8,128)(2,1)}, u32[]{:S(2)}, u32[]{:S(2)}) async-start(bf16[896,16,256]{2,0,1:T(8,128)(2,1)} %bitcast.28), calls=%async_computation | async-start | bytes 14680064 | tf_op jit(solution)/shard_map/all_to_all | solution.py:40
  20.9 294.6 %all-gather.3.cloned.1.call-start = ((), (), s32[]{:S(2)}) async-start(), calls=%async_computation.1 | async-start | bytes 15597568 | tf_op jit(solution)/shard_map/all_gather | solution.py:16
  326.6 2.6 copy-start
  326.6 2.6 copy-start.1
Sparse Core Ops, SparseCore 0:
  174.0 141.4 all-gather.2
